TPU v7x, 256 devices: a whole 4x4x8 slice. The times are simulated.
256 devices in a mesh: row: 8 (over z_lo, core), col: 32 (over z_hi, y, x).
Axes of the slice: x: 4, y: 4, z: 8 (z_hi: 2, z_lo: 4; z = z_hi * 4 + z_lo), core: 2. Of those that a mesh axis runs over, the one named last changes fastest.
Arguments:
- tokens: bfloat16 [1024, 12288], P('col', 'row'), may hold values from -6 to 6
- up_weight: bfloat16 [12288, 24576], P('row', 'col'), may hold values from -0.109375 to 0.109375
- down_weight: bfloat16 [24576, 12288], P('col', 'row'), may hold values from -0.078125 to 0.078125
- cotangent: bfloat16 [1024, 12288], P('col', 'row'), may hold values from -6 to 6
- up_pattern: int32 [96, 192], P('row', 'col'), may hold values 0 or 1
- down_pattern: int32 [192, 96], P('col', 'row'), may hold values 0 or 1
Outputs:
- input_grad: bfloat16 [1024, 12288], P('col', 'row')
- up_grad: bfloat16 [12288, 24576], P('row', 'col')
- down_grad: bfloat16 [24576, 12288], P('col', 'row')
All inputs are finite; a program needn't handle non-finite values. No bound on the sum of `up_pattern` or of `down_pattern` on one device may be relied on, other than what follows from the above.
Results may differ from a plain program's by a relative error of at most 0.015.
Values may be sent and summed in bfloat16 or wider, within the bound.
A program may use at most 128 MiB of HBM per device.

v0:
```python
import jax
import jax.numpy as jnp
from jax import lax
from jax.sharding import PartitionSpec as P

half_root = 0.7071067811865476
inv_root_tau = 0.3989422804014327


def widen(pattern, height, breadth):
    blocks_down, blocks_across = pattern.shape
    spread = pattern.astype(jnp.bfloat16)[:, None, :, None]
    spread = jnp.broadcast_to(
        spread, (blocks_down, height // blocks_down, blocks_across, breadth // blocks_across)
    )
    return spread.reshape(height, breadth)


def activate(pre, dact):
    cdf = 0.5 * (1.0 + jax.scipy.special.erf(pre * half_root))
    dens = jnp.exp(-0.5 * pre * pre) * inv_root_tau
    active = (pre * cdf).astype(jnp.bfloat16)
    dhid = (dact * (cdf + pre * dens)).astype(jnp.bfloat16)
    return (active, dhid)


def on_device(tokens, up_weight, down_weight, cotangent, up_pattern, down_pattern):
    full_tokens, full_cotangent = (
        lax.all_gather(tokens, "col", axis=0, tiled=True),
        lax.all_gather(cotangent, "col", axis=0, tiled=True),
    )
    up_mask = widen(up_pattern, up_weight.shape[0], up_weight.shape[1])
    down_mask = widen(down_pattern, down_weight.shape[0], down_weight.shape[1])
    up_eff = up_weight * up_mask
    down_eff = down_weight * down_mask
    pre_part = jnp.dot(full_tokens, up_eff, preferred_element_type=jnp.float32)
    dact_part = lax.dot_general(
        full_cotangent, down_eff, (((1,), (1,)), ((), ())), preferred_element_type=jnp.float32
    )
    pre, dact = lax.psum((pre_part, dact_part), "row")
    active, dhid = activate(pre, dact)
    input_grad = lax.psum_scatter(
        lax.dot_general(
            dhid, up_eff, (((1,), (1,)), ((), ())), preferred_element_type=jnp.float32
        ).astype(jnp.bfloat16),
        "col",
        scatter_dimension=0,
        tiled=True,
    )
    factor = 1.0 / jnp.sqrt(jnp.float32(full_tokens.shape[0]))
    up_grad = lax.dot_general(
        full_tokens, dhid, (((0,), (0,)), ((), ())), preferred_element_type=jnp.float32
    )
    up_grad = (up_grad * up_mask.astype(jnp.float32) * factor).astype(jnp.bfloat16)
    down_grad = lax.dot_general(
        active, full_cotangent, (((0,), (0,)), ((), ())), preferred_element_type=jnp.float32
    )
    down_grad = (down_grad * down_mask.astype(jnp.float32) * factor).astype(jnp.bfloat16)
    return (input_grad, up_grad, down_grad)


def solution(mesh):
    return jax.shard_map(
        on_device,
        mesh=mesh,
        in_specs=(
            P("col", "row"),
            P("row", "col"),
            P("col", "row"),
            P("col", "row"),
            P("row", "col"),
            P("col", "row"),
        ),
        out_specs=(P("col", "row"), P("row", "col"), P("col", "row")),
        check_vma=False,
    )
```

profile of v0, /device:TPU:2, one launch (start us, length us, event | category | flops | bytes accessed | tf_op | source)
XLA Modules:
  0.0 640.0 jit_solution(1797469134917920429)
XLA Ops:
  7.2 0.7 all-gather.5.cloned.1.call-update
  7.9 0.7 all-gather.3.cloned.1.call-update
  8.7 0.7 convert_element_type.28
  9.5 0.9 convert_element_type.27
  10.3 0.5 broadcast_in_dim.5
  10.8 0.4 copy-done.2
  11.2 1.7 fusion.11
  12.9 101.2 %all-gather.5.cloned.1.call-done = bf16[1024,1536]{1,0:T(8,128)(2,1)} async-done(((bf16[32,1536]{1,0:T(8,128)(2,1)}), bf16[1024,1536]{1,0:T(8,128)(2,1)}) %all-gather.5.cloned.1.call-update) | async-done | bytes 3145744 | tf_op jit(solution)/shard_map/all_gather | solution.py:29
  114.1 6.9 %convolution_bitcast_fusion = f32[1024,768]{0,1:T(8,128)} fusion(bf16[1536,768]{1,0:T(8,128)(2,1)} %get-tuple-element.11, bf16[1024,1536]{1,0:T(8,128)(2,1)} %all-gather.5.cloned.1.call-done), kind=kOutput, calls=%fused_computation.18 | convolution fusion | flops 2415919104 | bytes 8650752 | tf_op jit(solution)/shard_map/dot_general | solution.py:36
  121.0 91.3 %all-gather.3.cloned.1.call-done = bf16[1024,1536]{1,0:T(8,128)(2,1)} async-done(((bf16[32,1536]{1,0:T(8,128)(2,1)}), bf16[1024,1536]{1,0:T(8,128)(2,1)}) %all-gather.3.cloned.1.call-update) | async-done | bytes 3145744 | tf_op jit(solution)/shard_map/all_gather | solution.py:30
  212.3 0.5 broadcast_in_dim.4
  212.7 1.7 copy-done
  214.5 0.8 copy-done.5
  215.3 6.0 fusion.9
  221.3 0.2 reduce-scatter.2.cloned.1.call-start
  221.5 143.6 %all-reduce.3.cloned.1.call-done = (f32[1024,768]{0,1:T(8,128)}, f32[1024,768]{0,1:T(8,128)}) async-done(((f32[1024,768]{0,1:T(8,128)}, f32[1024,768]{0,1:T(8,128)}), (f32[1024,768]{0,1:T(8,128)}, f32[1024,768]{0,1:T(8,128)})) %all-reduce.3.cloned.1.call-update) | async-done | bytes 6291472 | tf_op jit(solution)/shard_map/psum | solution.py:40
  365.1 3.6 fusion.7
  368.8 1.1 copy-done.4
  369.9 4.1 convolution_convert_fusion
  374.1 2.4 copy.12
  376.5 7.1 %fusion.1 = bf16[1536,768]{0,1:T(8,128)(2,1)} fusion(bf16[1536,768]{0,1:T(8,128)(2,1)} %copy.12, bf16[1024,768]{0,1:T(8,128)(2,1)} %copy-done.4, bf16[1024,1536]{1,0:T(8,128)(2,1)} %all-gather.5.cloned.1.call-done), kind=kOutput, calls=%fused_computation.3 | convolution fusion | flops 2420637696 | bytes 9437184 | tf_op jit(solution)/shard_map/dot_general | solution.py:51
  383.6 4.4 copy.13
  388.0 6.9 %multiply_convert_fusion = bf16[768,1536]{1,0:T(8,128)(2,1)} fusion(bf16[1024,1536]{1,0:T(8,128)(2,1)} %all-gather.3.cloned.1.call-done, bf16[96,8,12,128]{3,2,1,0:T(8,128)(2,1)S(1)} %bitcast.33, f32[1024,768]{0,1:T(8,128)} %get-tuple-element.10), kind=kOutput, calls=%fused_computation.4 | convolution fusion | flops 2424569856 | bytes 11010048 | tf_op jit(solution)/shard_map/dot_general | solution.py:55
  394.9 238.5 %reduce-scatter.2.cloned.1.call-done = bf16[32,1536]{1,0:T(8,128)(2,1)} async-done(((bf16[1024,1536]{1,0:T(8,128)(2,1)}), bf16[32,1536]{1,0:T(8,128)(2,1)}) %reduce-scatter.2.cloned.1.call-update) | async-done | bytes 98320 | tf_op jit(solution)/shard_map/reduce_scatter | solution.py:42
  (14 shorter events, 0.3 us)
Async XLA Ops:
  7.2 106.9 %all-gather.5.cloned.1.call-start = ((), (), s32[]{:S(2)}) async-start(), calls=%async_computation.2 | async-start | bytes 3244032 | tf_op jit(solution)/shard_map/all_gather | solution.py:29
  7.9 204.4 %all-gather.3.cloned.1.call-start = ((), (), s32[]{:S(2)}) async-start(), calls=%async_computation.1 | async-start | bytes 3244032 | tf_op jit(solution)/shard_map/all_gather | solution.py:30
  8.6 356.5 %all-reduce.3.cloned.1.call-start = ((), (), s32[]{:S(2)}) async-start(), calls=%async_computation.4 | async-start | bytes 12582912 | tf_op jit(solution)/shard_map/psum | solution.py:40
  9.5 1.7 copy-start.2
  212.3 3.0 copy-start.5
  212.7 1.7 copy-start
  221.3 412.1 %reduce-scatter.2.cloned.1.call-start = ((), (), s32[]{:S(2)}) async-start(), calls=%async_computation.3 | async-start | bytes 3244032 | tf_op jit(solution)/shard_map/reduce_scatter | solution.py:42
  365.1 4.8 copy-start.3
  368.8 1.1 copy-start.4
  383.6 4.4 copy-start.1
Sparse Core Ops, SparseCore 0:
  11.5 102.5 all-gather.4
  117.5 94.6 all-gather.2
  221.4 143.6 all-reduce.2
  374.2 259.1 reduce-scatter.1
where the time goes:
time: 640 us
  waiting for transfers between devices  576 us (90%)
  matrix products  31.1 us (5%)
  between operations  13.8 us (2%)
  local copies, waits for them, and re-layouts  11.9 us (2%)
  other arithmetic  6.89 us (1%)
    reduce_scatter x1, waiting for transfers between devices, on_device(): lax.psum_scatter(lax.dot_general(dhid, up_eff, (((1,), (1,)), ((), ())),...  238 us
    psum x1, waiting for transfers between devices, on_device(): pre, dact = lax.psum((pre_part, dact_part), 'row')  144 us
    all_gather x1, waiting for transfers between devices, on_device(): lax.all_gather(tokens, 'col', axis=0, tiled=True)  101 us
    all_gather x1, waiting for transfers between devices, on_device(): lax.all_gather(cotangent, 'col', axis=0, tiled=True)  91.3 us
  transfers between devices with their start and end apart: 4, of which 4 were waited for; matrix products, arithmetic and copies ran while one was open for 5% of the time, Pallas kernels for 0%

commit v1 on v0

v1 whole, which is shorter than its diff:
```python
import jax
import jax.numpy as jnp
from jax import lax
from jax.experimental import pallas as pl
from jax.experimental.pallas import tpu as pltpu
from jax.sharding import PartitionSpec as P

MESH = pl.DeviceIdType.MESH
HALF_ROOT = 0.7071067811865476
INV_ROOT_TAU = 0.3989422804014327
BF = jnp.bfloat16
F32 = jnp.float32
NT = (((1,), (1,)), ((), ()))
TN = (((0,), (0,)), ((), ()))


def kernel(
    tok, upw, dnw, cot, upp, dnp, ig_out, ug_out, dg_out,
    T, G, U, D, PS, XS, XR, RSS, RSR, AD, IG, RA, RB, CS, R1, R1B, RC, RD, CS2, R2, ZS, ZR, UG, DG, OUT,
    lsem, ags, agr, zxs, zxr, xs, xr, rss, rsr, ads, adr, acs, acr, igs, igr, zss, zsr,
):
    r = lax.axis_index("row")
    q = lax.axis_index("col")
    zl, c = r // 2, lax.rem(r, 2)
    zh = q // 16
    y = lax.rem(q // 4, 4)
    x = lax.rem(q, 4)
    oc = 1 - c

    def m4(v):
        return lax.rem(v, 4)

    xp = (r, zh * 16 + y * 4 + m4(x + 1))
    xm = (r, zh * 16 + y * 4 + m4(x + 3))
    yp = (r, zh * 16 + m4(y + 1) * 4 + x)
    ym = (r, zh * 16 + m4(y + 3) * 4 + x)
    zz = (r, (1 - zh) * 16 + y * 4 + x)
    co = (zl * 2 + oc, q)
    zp = (m4(zl + 1) * 2 + c, q)
    zm = (m4(zl + 3) * 2 + c, q)

    o0 = m4(x + y)
    locals_ = [
        pltpu.make_async_copy(tok, T.at[0, o0, :, y], lsem.at[0]),
        pltpu.make_async_copy(cot, G.at[0, o0, :, y], lsem.at[1]),
        pltpu.make_async_copy(upw, U, lsem.at[2]),
        pltpu.make_async_copy(dnw, D, lsem.at[3]),
    ]
    for d in locals_:
        d.start()

    barrier = pltpu.get_barrier_semaphore()
    for dev in (xp, xm, yp, ym, zz, co, zp, zm):
        pl.semaphore_signal(barrier, inc=1, device_id=dev, device_id_type=MESH)
    locals_[0].wait()
    locals_[1].wait()
    pl.semaphore_wait(barrier, 8)

    pending = []

    def rcopy(src, dst, ss, rs, dev):
        return pltpu.make_async_remote_copy(
            src_ref=src, dst_ref=dst, send_sem=ss, recv_sem=rs, device_id=dev, device_id_type=MESH
        )

    def send(make, cond=None):
        if cond is None:
            make().start()
        else:
            @pl.when(cond)
            def _():
                make().start()
        pending.append((cond, make))

    def arrive(ref, ss, rs):
        rcopy(ref, ref, ss, rs, co).wait_recv()

    class Gather:
        def __init__(self, A, arr, rho):
            self.A, self.arr, self.rho = A, arr, rho
            self.fp, self.fm, self.sp, self.sm = (xp, xm, yp, ym) if arr == 0 else (yp, ym, xp, xm)

        def ref(self, da, db, h=None):
            da, db = da % 4, db % 4
            xx, yy = (m4(x + da), m4(y + db)) if self.arr == 0 else (m4(x + db), m4(y + da))
            o = m4(xx + yy)
            if h is None:
                return self.A.at[self.rho, o, :, yy]
            return self.A.at[self.rho, o, h, yy]

        def put(self, k, ref, dev):
            ss, rs = ags.at[self.arr, self.rho, k], agr.at[self.arr, self.rho, k]
            send(lambda: rcopy(ref, ref, ss, rs, dev))

        def get(self, k, ref):
            arrive(ref, ags.at[self.arr, self.rho, k], agr.at[self.arr, self.rho, k])

        def start(self):
            own = self.ref(0, 0)
            self.put(0, own, self.fp)
            self.put(1, own, self.fm)
            self.put(2, own, self.sp)
            self.put(3, own, self.sm)

        def step2(self):
            self.get(0, self.ref(-1, 0))
            self.put(4, self.ref(-1, 0, 0), self.fp)
            self.put(5, self.ref(-1, 0), self.sp)
            self.put(6, self.ref(-1, 0), self.sm)
            self.get(1, self.ref(1, 0))
            self.put(7, self.ref(1, 0, 1), self.fm)
            self.put(8, self.ref(1, 0), self.sp)
            self.put(9, self.ref(1, 0), self.sm)

        def step3(self):
            self.get(4, self.ref(2, 0, 0))
            self.get(7, self.ref(2, 0, 1))
            self.put(10, self.ref(2, 0), self.sp)
            self.put(11, self.ref(2, 0), self.sm)

        def step4a(self):
            self.get(2, self.ref(0, -1))
            self.put(12, self.ref(0, -1), self.sp)
            self.get(6, self.ref(-1, 1))
            self.put(13, self.ref(-1, 1), self.sm)

        def step4b(self):
            self.get(8, self.ref(1, -1))
            self.put(14, self.ref(1, -1), self.sp)
            self.get(11, self.ref(2, 1))
            self.put(15, self.ref(2, 1), self.sm)

        def finish(self):
            self.get(3, self.ref(0, 1))
            self.get(5, self.ref(-1, -1))
            self.get(9, self.ref(1, 1))
            self.get(10, self.ref(2, -1))
            self.get(12, self.ref(0, 2))
            self.get(13, self.ref(-1, 2))
            self.get(14, self.ref(1, 2))
            self.get(15, self.ref(2, 2))

    gt0, gg0 = Gather(T, 0, 0), Gather(G, 1, 0)
    gt1, gg1 = Gather(T, 0, 1), Gather(G, 1, 1)

    def across(A, k):
        src, dst = A.at[0, o0, :, y], A.at[1, o0, :, y]
        send(lambda: rcopy(src, dst, zxs.at[k], zxr.at[k], zz))

    def across_wait(A, k):
        arrive(A.at[1, o0, :, y], zxs.at[k], zxr.at[k])

    def row_a(i):
        rho, f = i // 3, i % 3
        cols = slice(f * 256, (f + 1) * 256)
        for o in range(0, 4, 2):
            t = T[rho, o:o + 2].reshape(256, 1536)
            pre = jnp.dot(t, U[:, cols], preferred_element_type=F32)
            PS[i, 0, o:o + 2] = pre.reshape(2, 2, 4, 16, 256)
            g = G[rho, o:o + 2].reshape(256, 1536)
            dact = lax.dot_general(g, D[cols, :], NT, preferred_element_type=F32)
            PS[i, 1, o:o + 2] = dact.reshape(2, 2, 4, 16, 256)
        XS[i] = PS[i, :, :, oc].astype(BF)
        send(lambda: rcopy(XS.at[i], XR.at[i], xs.at[i], xr.at[i], co))

    def rs_send(i, way, k, cond):
        dev = zp if way == 0 else zm
        send(
            lambda: rcopy(
                RSS.at[i, way, k - 1], RSR.at[i, way, k - 1], rss.at[i, way, k - 1], rsr.at[i, way, k - 1], dev
            ),
            cond,
        )

    def rs_arrive(i, way, k):
        arrive(RSR.at[i, way, k - 1], rss.at[i, way, k - 1], rsr.at[i, way, k - 1])

    def row_b(i):
        arrive(XR.at[i], xs.at[i], xr.at[i])
        PS[i, :, :, c] = PS[i, :, :, c] + XR[i].astype(F32)

        @pl.when(zl == 0)
        def _():
            for k in (3, 2, 1):
                RSS[i, 0, k - 1] = PS[i, :, k, c].astype(BF)

        @pl.when(zl == 3)
        def _():
            for k in (3, 2, 1):
                RSS[i, 1, k - 1] = PS[i, :, 3 - k, c].astype(BF)

        for k in (3, 2, 1):
            rs_send(i, 0, k, zl == 0)
            rs_send(i, 1, k, zl == 3)

    def row_c(i, k):
        right = jnp.logical_and(zl >= 1, zl + k <= 3)
        left = jnp.logical_and(zl <= 2, zl - k >= 0)

        @pl.when(right)
        def _():
            rs_arrive(i, 0, k + 1)
            RSS[i, 0, k - 1] = (PS[i, :, zl + k, c] + RSR[i, 0, k].astype(F32)).astype(BF)

        rs_send(i, 0, k, right)

        @pl.when(left)
        def _():
            rs_arrive(i, 1, k + 1)
            RSS[i, 1, k - 1] = (PS[i, :, zl - k, c] + RSR[i, 1, k].astype(F32)).astype(BF)

        rs_send(i, 1, k, left)

    has_left, has_right = zl >= 1, zl <= 2

    def ad_line(i, way, d, block, cond):
        dev = zp if way == 0 else zm
        f_rho = (i // 3, i % 3)
        send(
            lambda: rcopy(
                AD.at[f_rho[0], f_rho[1], block, c], AD.at[f_rho[0], f_rho[1], block, c],
                ads.at[i, way, d - 1], adr.at[i, way, d - 1], dev,
            ),
            cond,
        )

    def ad_core(i, slot, block, cond):
        send(
            lambda: rcopy(
                AD.at[i // 3, i % 3, block, c], AD.at[i // 3, i % 3, block, c], acs.at[i, slot], acr.at[i, slot], co
            ),
            cond,
        )

    def row_d(i):
        rho, f = i // 3, i % 3

        @pl.when(has_left)
        def _():
            rs_arrive(i, 0, 1)
            PS[i, :, zl, c] = PS[i, :, zl, c] + RSR[i, 0, 0].astype(F32)

        @pl.when(has_right)
        def _():
            rs_arrive(i, 1, 1)
            PS[i, :, zl, c] = PS[i, :, zl, c] + RSR[i, 1, 0].astype(F32)

        pre = PS[i, 0, zl, c]
        dact = PS[i, 1, zl, c]
        cdf = 0.5 * (1.0 + lax.erf(pre * HALF_ROOT))
        dens = jnp.exp(-0.5 * pre * pre) * INV_ROOT_TAU
        AD[rho, f, zl, c, 0] = (pre * cdf).astype(BF)
        AD[rho, f, zl, c, 1] = (dact * (cdf + pre * dens)).astype(BF)
        ad_line(i, 0, 1, zl, has_right)
        ad_line(i, 1, 1, zl, has_left)
        ad_core(i, 0, zl, None)

    def row_e(i, d):
        from_left, from_right = zl - d >= 0, zl + d <= 3

        @pl.when(from_left)
        def _():
            arrive(AD.at[i // 3, i % 3, zl - d, c], ads.at[i, 0, d - 1], adr.at[i, 0, d - 1])

        if d < 3:
            ad_line(i, 0, d + 1, zl - d, jnp.logical_and(from_left, has_right))
        ad_core(i, d, zl - d, from_left)

        @pl.when(from_right)
        def _():
            arrive(AD.at[i // 3, i % 3, zl + d, c], ads.at[i, 1, d - 1], adr.at[i, 1, d - 1])

        if d < 3:
            ad_line(i, 1, d + 1, zl + d, jnp.logical_and(from_right, has_left))
        ad_core(i, 3 + d, zl + d, from_right)

    def row_f(i):
        arrive(AD.at[i // 3, i % 3, zl, oc], acs.at[i, 0], acr.at[i, 0])
        for d in (1, 2, 3):
            @pl.when(zl - d >= 0)
            def _():
                arrive(AD.at[i // 3, i % 3, zl - d, oc], acs.at[i, d], acr.at[i, d])

            @pl.when(zl + d <= 3)
            def _():
                arrive(AD.at[i // 3, i % 3, zl + d, oc], acs.at[i, 3 + d], acr.at[i, 3 + d])

    def ig_matmul(rho, h):
        @pl.loop(0, 3)
        def _(n):
            rows = pl.ds(pl.multiple_of(h * 768 + n * 256, 256), 256)
            cols = pl.ds(pl.multiple_of(n * 256, 256), 256)
            for o in range(0, 4, 2):
                acc = jnp.zeros((256, 256), F32)
                for f in range(3):
                    dh = AD[rho, f, o:o + 2, :, 1].reshape(256, 256)
                    acc = acc + lax.dot_general(
                        dh, U[rows, f * 256:(f + 1) * 256], NT, preferred_element_type=F32
                    )
                acc = acc.astype(BF).reshape(2, 2, 4, 16, 256)
                for oo in range(2):
                    for yy in range(4):
                        xx = (o + oo - yy) % 4
                        a, b = (yy, xx) if h == 0 else (xx, yy)
                        IG[rho, h, a, b, :, :, cols] = acc[oo, :, yy]

    class Scatter:
        def __init__(self, rho, h):
            self.rho, self.h = rho, h
            self.fp, self.fm, self.sp, self.sm = (yp, ym, xp, xm) if h == 0 else (xp, xm, yp, ym)
            self.a, self.b = (y, x) if h == 0 else (x, y)

        def put(self, k, src, dst, dev):
            ss, rs = igs.at[self.rho, self.h, k], igr.at[self.rho, self.h, k]
            send(lambda: rcopy(src, dst, ss, rs, dev))

        def get(self, k, ref):
            arrive(ref, igs.at[self.rho, self.h, k], igr.at[self.rho, self.h, k])

        def start(self):
            i = (self.rho, self.h)
            a = self.a
            a1, a2, a3 = m4(a + 1), m4(a + 2), m4(a + 3)
            self.put(0, IG.at[i[0], i[1], a2, 0:2], RA.at[i[0], i[1], 0], self.fp)
            self.put(1, IG.at[i[0], i[1], a2, 2:4], RA.at[i[0], i[1], 1], self.fm)
            self.put(2, IG.at[i[0], i[1], a1, 2:4], RB.at[i[0], i[1], 0, 2:4], self.fp)
            self.put(3, IG.at[i[0], i[1], a3, 0:2], RB.at[i[0], i[1], 1, 0:2], self.fm)

        def step2(self):
            rho, h, a = self.rho, self.h, self.a
            a1, a3 = m4(a + 1), m4(a + 3)
            self.get(0, RA.at[rho, h, 0])
            CS[rho, h, 0] = (IG[rho, h, a1, 0:2].astype(F32) + RA[rho, h, 0].astype(F32)).astype(BF)
            self.put(4, CS.at[rho, h, 0], RB.at[rho, h, 0, 0:2], self.fp)
            self.get(1, RA.at[rho, h, 1])
            CS[rho, h, 1] = (IG[rho, h, a3, 2:4].astype(F32) + RA[rho, h, 1].astype(F32)).astype(BF)
            self.put(5, CS.at[rho, h, 1], RB.at[rho, h, 1, 2:4], self.fm)

        def step3(self):
            rho, h, a, b = self.rho, self.h, self.a, self.b
            self.get(2, RB.at[rho, h, 0, 2:4])
            self.get(3, RB.at[rho, h, 1, 0:2])
            self.get(4, RB.at[rho, h, 0, 0:2])
            self.get(5, RB.at[rho, h, 1, 2:4])
            for k in range(4):
                s = IG[rho, h, a, k].astype(F32) + RB[rho, h, 0, k].astype(F32) + RB[rho, h, 1, k].astype(F32)
                R1[rho, h, k] = s
                R1B[rho, h, k] = s.astype(BF)
            b1, b2, b3 = m4(b + 1), m4(b + 2), m4(b + 3)
            self.put(6, R1B.at[rho, h, b2, 0], RC.at[rho, h, 0], self.sp)
            self.put(7, R1B.at[rho, h, b2, 1], RC.at[rho, h, 1], self.sm)
            self.put(8, R1B.at[rho, h, b1, 1], RD.at[rho, h, 0, 1], self.sp)
            self.put(9, R1B.at[rho, h, b3, 0], RD.at[rho, h, 1, 0], self.sm)

        def step4(self):
            rho, h, b = self.rho, self.h, self.b
            b1, b3 = m4(b + 1), m4(b + 3)
            self.get(6, RC.at[rho, h, 0])
            CS2[rho, h, 0] = (R1[rho, h, b1, 0] + RC[rho, h, 0].astype(F32)).astype(BF)
            self.put(10, CS2.at[rho, h, 0], RD.at[rho, h, 0, 0], self.sp)
            self.get(7, RC.at[rho, h, 1])
            CS2[rho, h, 1] = (R1[rho, h, b3, 1] + RC[rho, h, 1].astype(F32)).astype(BF)
            self.put(11, CS2.at[rho, h, 1], RD.at[rho, h, 1, 1], self.sm)

        def step5(self):
            rho, h, b = self.rho, self.h, self.b
            self.get(8, RD.at[rho, h, 0, 1])
            self.get(9, RD.at[rho, h, 1, 0])
            self.get(10, RD.at[rho, h, 0, 0])
            self.get(11, RD.at[rho, h, 1, 1])
            s = R1[rho, h, b] + RD[rho, h, 0].astype(F32) + RD[rho, h, 1].astype(F32)
            if rho == 0:
                R2[h] = s
            else:
                ZS[h] = s.astype(BF)
                send(lambda: rcopy(ZS.at[h], ZR.at[h], zss.at[h], zsr.at[h], zz))

        def out(self):
            h = self.h
            arrive(ZR.at[h], zss.at[h], zsr.at[h])
            OUT[:, h * 768:(h + 1) * 768] = (R2[h] + ZR[h].astype(F32)).astype(BF).reshape(32, 768)

    sc = [[Scatter(rho, h) for h in range(2)] for rho in range(2)]

    def mask_weights():
        @pl.loop(0, 12)
        def _(i):
            rows = pl.ds(pl.multiple_of(i * 128, 128), 128)
            for j in range(6):
                cols = slice(j * 128, (j + 1) * 128)
                m = upp[i, j].astype(F32)
                U[rows, cols] = (U[rows, cols].astype(F32) * m).astype(BF)

        @pl.loop(0, 12)
        def _(i):
            cols = pl.ds(pl.multiple_of(i * 128, 128), 128)
            for j in range(6):
                rows = slice(j * 128, (j + 1) * 128)
                m = dnp[j, i].astype(F32)
                D[rows, cols] = (D[rows, cols].astype(F32) * m).astype(BF)

    factor = 1.0 / 32.0

    def up_grads(lo, hi):
        @pl.loop(lo, hi)
        def _(n):
            cols = pl.ds(pl.multiple_of(n * 256, 256), 256)
            t = T[:, :, :, :, :, cols].reshape(1024, 256)
            for f in range(3):
                dh = AD[:, f, :, :, 1].reshape(1024, 256)
                res = lax.dot_general(t, dh, TN, preferred_element_type=F32)
                for bi in range(2):
                    for bj in range(2):
                        m = upp[n * 2 + bi, f * 2 + bj].astype(F32) * factor
                        UG[
                            pl.ds(pl.multiple_of(n * 256 + bi * 128, 128), 128),
                            f * 256 + bj * 128:f * 256 + (bj + 1) * 128,
                        ] = (res[bi * 128:(bi + 1) * 128, bj * 128:(bj + 1) * 128] * m).astype(BF)

    def down_grads(lo, hi):
        @pl.loop(lo, hi)
        def _(n):
            cols = pl.ds(pl.multiple_of(n * 256, 256), 256)
            g = G[:, :, :, :, :, cols].reshape(1024, 256)
            for f in range(3):
                ac = AD[:, f, :, :, 0].reshape(1024, 256)
                res = lax.dot_general(ac, g, TN, preferred_element_type=F32)
                for bi in range(2):
                    for bj in range(2):
                        m = dnp[f * 2 + bi, n * 2 + bj].astype(F32) * factor
                        DG[
                            f * 256 + bi * 128:f * 256 + (bi + 1) * 128,
                            pl.ds(pl.multiple_of(n * 256 + bj * 128, 128), 128),
                        ] = (res[bi * 128:(bi + 1) * 128, bj * 128:(bj + 1) * 128] * m).astype(BF)

    gt0.start()
    gg0.start()
    across(T, 0)
    across(G, 1)
    locals_[2].wait()
    locals_[3].wait()
    mask_weights()
    gt0.step2()
    gg0.step2()
    gt0.step3()
    gg0.step3()
    gt0.step4a()
    gg0.step4a()
    gt0.step4b()
    gg0.step4b()
    across_wait(T, 0)
    gt1.start()
    across_wait(G, 1)
    gg1.start()
    gt0.finish()
    gg0.finish()

    def burst(rho, extra):
        i0 = rho * 3
        stages = [row_a, row_b, lambda i: row_c(i, 2), lambda i: row_c(i, 1), row_d,
                  lambda i: row_e(i, 1), lambda i: row_e(i, 2), lambda i: row_e(i, 3), row_f]
        for t in range(11):
            order = range(3)
            for f in order:
                s = t - f
                if 0 <= s < 9:
                    stages[s](i0 + f)
            for fn in extra.get(t, ()):
                fn()

    burst(0, {
        1: (gt1.step2, gg1.step2),
        3: (gt1.step3, gg1.step3),
        5: (gt1.step4a, gg1.step4a),
        7: (gt1.step4b, gg1.step4b),
    })
    gt1.finish()
    gg1.finish()

    def both(rho, name):
        def run():
            for h in range(2):
                getattr(sc[rho][h], name)()
        return run

    def ig0():
        for h in range(2):
            ig_matmul(0, h)
            sc[0][h].start()

    burst(1, {
        2: (ig0,),
        4: (both(0, "step2"),),
        5: (both(0, "step3"),),
        7: (both(0, "step4"),),
        8: (both(0, "step5"),),
    })
    for h in range(2):
        ig_matmul(1, h)
        sc[1][h].start()
    up_grads(0, 3)
    both(1, "step2")()
    up_grads(3, 6)
    both(1, "step3")()
    down_grads(0, 2)
    both(1, "step4")()
    down_grads(2, 4)
    both(1, "step5")()
    up_copy = pltpu.make_async_copy(UG, ug_out, lsem.at[0])
    up_copy.start()
    down_grads(4, 6)
    dn_copy = pltpu.make_async_copy(DG, dg_out, lsem.at[1])
    dn_copy.start()
    for h in range(2):
        sc[0][h].out()
    ig_copy = pltpu.make_async_copy(OUT, ig_out, lsem.at[2])
    ig_copy.start()

    for cond, make in pending:
        if cond is None:
            make().wait_send()
        else:
            @pl.when(cond)
            def _():
                make().wait_send()
    up_copy.wait()
    dn_copy.wait()
    ig_copy.wait()


def on_device(tokens, up_weight, down_weight, cotangent, up_pattern, down_pattern):
    any_ = pl.BlockSpec(memory_space=pl.ANY)
    smem = pl.BlockSpec(memory_space=pltpu.SMEM)
    dma = pltpu.SemaphoreType.DMA
    V = pltpu.VMEM
    return pl.pallas_call(
        kernel,
        out_shape=(
            jax.ShapeDtypeStruct((32, 1536), BF),
            jax.ShapeDtypeStruct((1536, 768), BF),
            jax.ShapeDtypeStruct((768, 1536), BF),
        ),
        in_specs=[any_, any_, any_, any_, smem, smem],
        out_specs=(any_, any_, any_),
        scratch_shapes=[
            V((2, 4, 2, 4, 16, 1536), BF),
            V((2, 4, 2, 4, 16, 1536), BF),
            V((1536, 768), BF),
            V((768, 1536), BF),
            V((6, 2, 4, 2, 4, 16, 256), F32),
            V((6, 2, 4, 4, 16, 256), BF),
            V((6, 2, 4, 4, 16, 256), BF),
            V((6, 2, 3, 2, 4, 16, 256), BF),
            V((6, 2, 3, 2, 4, 16, 256), BF),
            V((2, 3, 4, 2, 2, 4, 16, 256), BF),
            V((2, 2, 4, 4, 2, 16, 768), BF),
            V((2, 2, 2, 2, 2, 16, 768), BF),
            V((2, 2, 2, 4, 2, 16, 768), BF),
            V((2, 2, 2, 2, 2, 16, 768), BF),
            V((2, 2, 4, 2, 16, 768), F32),
            V((2, 2, 4, 2, 16, 768), BF),
            V((2, 2, 2, 16, 768), BF),
            V((2, 2, 2, 2, 16, 768), BF),
            V((2, 2, 2, 16, 768), BF),
            V((2, 2, 16, 768), F32),
            V((2, 2, 16, 768), BF),
            V((2, 2, 16, 768), BF),
            V((1536, 768), BF),
            V((768, 1536), BF),
            V((32, 1536), BF),
            dma((4,)),
            dma((2, 2, 16)), dma((2, 2, 16)),
            dma((2,)), dma((2,)),
            dma((6,)), dma((6,)),
            dma((6, 2, 3)), dma((6, 2, 3)),
            dma((6, 2, 3)), dma((6, 2, 3)),
            dma((6, 7)), dma((6, 7)),
            dma((2, 2, 12)), dma((2, 2, 12)),
            dma((2,)), dma((2,)),
        ],
        compiler_params=pltpu.CompilerParams(
            collective_id=0, has_side_effects=True, vmem_limit_bytes=62 * 1024 * 1024
        ),
    )(
        tokens.reshape(2, 16, 1536),
        up_weight,
        down_weight,
        cotangent.reshape(2, 16, 1536),
        up_pattern,
        down_pattern,
    )


def solution(mesh):
    return jax.shard_map(
        on_device,
        mesh=mesh,
        in_specs=(
            P("col", "row"),
            P("row", "col"),
            P("col", "row"),
            P("col", "row"),
            P("row", "col"),
            P("col", "row"),
        ),
        out_specs=(P("col", "row"), P("row", "col"), P("col", "row")),
        check_vma=False,
    )
```

time: 640 us -> 137 us (0.21)
  waiting for transfers between devices: 576 us -> 0 us
  Pallas kernels: 0 us -> 128 us
  matrix products: 31.1 us -> 0 us
  between operations: 13.8 us -> 0.64 us
  other arithmetic: 6.89 us -> 0 us
    reduce_scatter x1 -> x0, waiting for transfers between devices: 238 us -> none  [on_device(): lax.psum_scatter(lax.dot_general(dhid, up_eff, (((1,), (1,)), ((), ())),...]
    all_gather x2 -> x0, waiting for transfers between devices: 192 us -> none  [the longest x1 101 us: on_device(): lax.all_gather(tokens, 'col', axis=0, tiled=True)]
    psum x1 -> x0, waiting for transfers between devices: 144 us -> none  [on_device(): pre, dact = lax.psum((pre_part, dact_part), 'row')]
    pallas_call x0 -> x1, Pallas kernels: none -> 128 us  [on_device(): pl.pallas_call(kernel, out_shape=(jax.ShapeDtypeStruct((32, 1536), BF), j...]
    dot_general x5 -> x0, matrix products: 31.1 us -> none  [the longest x1 7.1 us: on_device(): lax.dot_general(full_tokens, dhid, (((0,), (0,)), ((), ())), preferred_el...]
  transfers between devices with their start and end apart: 4 -> 0, of which waited for: 4 -> 0; matrix products, arithmetic and copies ran while one was open for 5% -> 0% of each run, Pallas kernels for 0% -> 0%
where the time goes in v1:
time: 137 us
  Pallas kernels  128 us (93%)
  local copies, waits for them, and re-layouts  7.69 us (6%)
    pallas_call x1, Pallas kernels, on_device(): pl.pallas_call(kernel, out_shape=(jax.ShapeDtypeStruct((32, 1536), BF), j...  128 us
    unnamed x6, local copies, waits for them, and re-layouts  7.69 us

profile of v1, /device:TPU:2, one launch (start us, length us, event | category | flops | bytes accessed | tf_op | source)
XLA Modules:
  0.0 136.5 jit_solution(17538730501988512116)
XLA Ops:
  0.6 1.4 %copy.9.upp = s32[12,6]{1,0:T(8,128)} copy(s32[12,6]{0,1:T(8,128)} %param.10) | data formatting | bytes 576 | tf_op args[4]
  2.0 128.2 %shard_map.85 = (bf16[32,1536]{1,0:T(8,128)(2,1)}, bf16[1536,768]{1,0:T(8,128)(2,1)}, bf16[768,1536]{1,0:T(8,128)(2,1)}) custom-call(bf16[2,16,1536]{2,1,0:T(8,128)(2,1)} %bitcast.2, bf16[1536,768]{1,0:T(8,128)(2,1)} %upw.1, bf16[768,1536]{1,0:T(8,128)(2,1)} %dnw.1, bf16[2,16,1536]{2,1,0:T(8,128)(2,1)} %bitcast.3, s32[12,6]{1,0:T(8,128)} %copy.9.upp, ...), custom_call_target="tpu_custom_call" | custom-call | tf_op jit(solution)/shard_map/pallas_call | solution.py:536
  130.2 1.5 %copy.13 = bf16[32,1536]{1,0:T(8,128)(2,1)} copy(bf16[32,1536]{1,0:T(8,128)(2,1)} %get-tuple-element.6) | data formatting | bytes 196608
  131.7 0.0 copy-start
  131.7 3.4 %copy.14 = bf16[1536,768]{1,0:T(8,128)(2,1)} copy(bf16[1536,768]{1,0:T(8,128)(2,1)} %get-tuple-element.7) | data formatting | bytes 4718592
  135.1 0.0 copy-done
  135.1 1.4 %copy.15 = bf16[768,1536]{1,0:T(8,128)(2,1)} copy(bf16[768,1536]{1,0:T(8,128)(2,1)S(1)} %copy-done) | data formatting | bytes 4718592
Async XLA Ops:
  131.7 3.4 %copy-start = (bf16[768,1536]{1,0:T(8,128)(2,1)S(1)}, bf16[768,1536]{1,0:T(8,128)(2,1)}, u32[]{:S(2)}) copy-start(bf16[768,1536]{1,0:T(8,128)(2,1)} %get-tuple-element.8) | copy-start | bytes 7077892

commit v2 on v1

v2 whole, which is shorter than its diff:
```python
import jax
import jax.numpy as jnp
from jax import lax
from jax.experimental import pallas as pl
from jax.experimental.pallas import tpu as pltpu
from jax.sharding import PartitionSpec as P

MESH = pl.DeviceIdType.MESH
HALF_ROOT = 0.7071067811865476
INV_ROOT_TAU = 0.3989422804014327
BF = jnp.bfloat16
F32 = jnp.float32
NT = (((1,), (1,)), ((), ()))
TN = (((0,), (0,)), ((), ()))

ORDER = (
    0, 11, 44, 45, 46, 1, 12, 2, 13, 3, 14, 17, 6, 4, 15, 5, 16, 49, 57, 18, 7, 47, 22, 48,
    33, 23, 34, 50, 58, 51, 54, 19, 8, 9, 20, 65, 73, 59, 62, 81, 89, 66, 52, 55, 74, 82, 90, 35,
    24, 25, 36, 60, 63, 67, 70, 53, 56, 21, 10, 97, 75, 78, 105, 61, 64, 114, 83, 86, 98, 91, 94, 68,
    71, 37, 200, 26, 27, 38, 106, 192, 28, 39, 76, 79, 115, 84, 87, 201, 29, 40, 102, 99, 193, 69, 72, 92,
    95, 169, 110, 107, 77, 80, 137, 30, 31, 41, 42, 208, 117, 216, 88, 202, 145, 205, 122, 85, 224, 103, 100, 194,
    154, 93, 197, 96, 232, 111, 121, 108, 209, 172, 217, 225, 119, 140, 32, 240, 43, 203, 206, 233, 123, 248, 104, 101,
    195, 198, 148, 155, 124, 112, 109, 174, 210, 241, 213, 249, 142, 218, 204, 207, 221, 125, 226, 150, 130, 196, 199, 229,
    157, 113, 234, 126, 138, 176, 237, 211, 129, 242, 214, 146, 144, 245, 219, 127, 153, 250, 222, 162, 152, 253, 227, 159,
    161, 131, 230, 170, 128, 116, 235, 212, 312, 139, 238, 257, 215, 132, 243, 220, 280, 147, 246, 223, 156, 251, 228, 288,
    163, 254, 231, 164, 133, 265, 236, 264, 297, 171, 118, 239, 315, 141, 244, 272, 281, 258, 134, 247, 283, 149, 252, 256,
    289, 158, 255, 291, 165, 135, 266, 296, 273, 166, 120, 267, 173, 143, 298, 304, 305, 317, 136, 275, 260, 151, 282, 313,
    160, 167, 285, 290, 259, 168, 268, 299, 175, 177, 178, 269, 274, 293, 319, 262, 306, 300, 284, 307, 179, 185, 277, 314,
    186, 292, 180, 287, 261, 276, 187, 271, 301, 270, 302, 295, 308, 309, 286, 181, 279, 316, 294, 188, 263, 278, 303, 310,
    311, 318, 320, 321, 322, 328, 329, 182, 189, 335, 337, 323, 339, 330, 341, 324, 190, 331, 343, 183, 345, 336, 325, 191,
    332, 338, 184, 340, 326, 333, 342, 327, 334, 344, 346, 347, 348,
)


def kernel(
    tok, upw, dnw, cot, upp, dnp, ig_out, ug_out, dg_out,
    T, G, U, D, DT, PS, XS, XR, RSS, RSR, AD, IG, RA, RB, CS, R1, R1B, RC, RD, CS2, R2, ZS, ZR, UG, DG, OUT,
    lsem, ags, agr, zxs, zxr, xss, xr, rss, rsr, ads, adr, acs, acr, igs, igr, zss, zsr,
):
    r = lax.axis_index("row")
    q = lax.axis_index("col")
    zl, c = r // 2, lax.rem(r, 2)
    zh = q // 16
    y = lax.rem(q // 4, 4)
    x = lax.rem(q, 4)
    oc = 1 - c

    def m4(v):
        return lax.rem(v, 4)

    xp = (r, zh * 16 + y * 4 + m4(x + 1))
    xm = (r, zh * 16 + y * 4 + m4(x + 3))
    yp = (r, zh * 16 + m4(y + 1) * 4 + x)
    ym = (r, zh * 16 + m4(y + 3) * 4 + x)
    zz = (r, (1 - zh) * 16 + y * 4 + x)
    co = (zl * 2 + oc, q)
    zp = (m4(zl + 1) * 2 + c, q)
    zm = (m4(zl + 3) * 2 + c, q)

    o0 = m4(x + y)
    locals_ = [
        pltpu.make_async_copy(tok, T.at[0, o0, :, y], lsem.at[0]),
        pltpu.make_async_copy(cot, G.at[0, o0, :, y], lsem.at[1]),
        pltpu.make_async_copy(upw, U, lsem.at[2]),
        pltpu.make_async_copy(dnw, D, lsem.at[3]),
    ]
    for d in locals_:
        d.start()

    barrier = pltpu.get_barrier_semaphore()
    for dev in (xp, xm, yp, ym, zz, co, zp, zm):
        pl.semaphore_signal(barrier, inc=1, device_id=dev, device_id_type=MESH)
    locals_[0].wait()
    locals_[1].wait()
    pl.semaphore_wait(barrier, 8)

    pending = []

    def rcopy(src, dst, ss, rs, dev):
        return pltpu.make_async_remote_copy(
            src_ref=src, dst_ref=dst, send_sem=ss, recv_sem=rs, device_id=dev, device_id_type=MESH
        )

    def send(make, cond=None):
        if cond is None:
            make().start()
        else:
            @pl.when(cond)
            def _():
                make().start()

    def arrive(ref, rs):
        rcopy(ref, ref, xss, rs, co).wait_recv()

    def sent(ref, ss, cond=None):
        pending.append((cond, lambda: rcopy(ref, ref, ss, zsr.at[0], co)))

    class Gather:
        def __init__(self, A, arr, rho):
            self.A, self.arr, self.rho = A, arr, rho
            self.fp, self.fm, self.sp, self.sm = (xp, xm, yp, ym) if arr == 0 else (yp, ym, xp, xm)
            sent(A.at[rho, 0, :, 0:3], ags.at[arr, rho, 0])
            sent(A.at[rho, 0:3], ags.at[arr, rho, 1])

        def ref(self, da, db, h=None):
            da, db = da % 4, db % 4
            xx, yy = (m4(x + da), m4(y + db)) if self.arr == 0 else (m4(x + db), m4(y + da))
            o = m4(xx + yy)
            if h is None:
                return self.A.at[self.rho, o, :, yy]
            return self.A.at[self.rho, o, h, yy]

        slots = {0: 0, 1: 1, 4: 2, 7: 2, 2: 3, 6: 4, 8: 5, 11: 6, 3: 7, 5: 7, 9: 7, 10: 7, 12: 8, 13: 8, 14: 8, 15: 8}

        def put(self, k, ref, dev):
            ss = ags.at[self.arr, self.rho, 0 if k in (0, 1, 4, 7) else 1]
            rs = agr.at[self.arr, self.rho, self.slots[k]]
            send(lambda: rcopy(ref, ref, ss, rs, dev))

        def get(self, k, ref):
            arrive(ref, agr.at[self.arr, self.rho, self.slots[k]])

        def start_a(self):
            own = self.ref(0, 0)
            self.put(0, own, self.fp)
            self.put(1, own, self.fm)

        def start_b(self):
            own = self.ref(0, 0)
            self.put(2, own, self.sp)
            self.put(3, own, self.sm)

        def step2a(self):
            self.get(0, self.ref(-1, 0))
            self.put(4, self.ref(-1, 0, 0), self.fp)
            self.get(1, self.ref(1, 0))
            self.put(7, self.ref(1, 0, 1), self.fm)

        def step2b(self):
            self.put(5, self.ref(-1, 0), self.sp)
            self.put(6, self.ref(-1, 0), self.sm)
            self.put(8, self.ref(1, 0), self.sp)
            self.put(9, self.ref(1, 0), self.sm)

        def step3(self):
            self.get(4, self.ref(2, 0))
            self.put(10, self.ref(2, 0), self.sp)
            self.put(11, self.ref(2, 0), self.sm)

        def step4a(self):
            self.get(2, self.ref(0, -1))
            self.put(12, self.ref(0, -1), self.sp)

        def step4b(self):
            self.get(6, self.ref(-1, 1))
            self.put(13, self.ref(-1, 1), self.sm)

        def step4c(self):
            self.get(8, self.ref(1, -1))
            self.put(14, self.ref(1, -1), self.sp)

        def step4d(self):
            self.get(11, self.ref(2, 1))
            self.put(15, self.ref(2, 1), self.sm)

        def near(self):
            self.get(3, self.A.at[self.rho, 0])

        def far(self):
            self.get(12, self.A.at[self.rho, 0])

    gt0, gg0 = Gather(T, 0, 0), Gather(G, 1, 0)
    gt1, gg1 = Gather(T, 0, 1), Gather(G, 1, 1)

    def across(A, k):
        src, dst = A.at[0, o0, :, y], A.at[1, o0, :, y]
        sent(src, zxs.at[k])
        send(lambda: rcopy(src, dst, zxs.at[k], zxr.at[k], zz))

    def across_wait(A, k):
        arrive(A.at[1, o0, :, y], zxr.at[k])

    shift = (0, 3, 1, 2)

    def slot(do):
        return m4(x + y + do)

    def shard_row(arr, g, do):
        if arr == 0:
            return m4(y + shift[g])
        return m4(slot(do) + 4 - m4(x + shift[g]))

    def row_a(rho, arr, g):
        A = G if arr else T
        t = jnp.concatenate([A[rho, slot(o), :, shard_row(arr, g, o)].reshape(32, 1536) for o in range(4)], axis=0)
        if arr == 0:
            p = jnp.dot(t, U[...], preferred_element_type=F32)
        else:
            p = jnp.dot(t, DT[...], preferred_element_type=F32)
        p = p.reshape(4, 2, 16, 768)
        for o in range(4):
            PS[rho, arr, slot(o), :, shard_row(arr, g, o)] = p[o]
        for o in range(4):
            XS[rho, arr, g, o] = PS[rho, arr, slot(o), oc, shard_row(arr, g, o)].astype(BF)
        send(lambda: rcopy(XS.at[rho, arr, g], XR.at[rho, arr, g], xss, xr.at[rho, arr, g], co))

    def block_of(way, j):
        return 2 + j if way == 0 else j

    def rs_pass(rho, arr, g, way):
        dev = zp if way == 0 else zm
        k = (rho, arr, g, way)
        return lambda: rcopy(RSS.at[k], RSR.at[k], rss.at[way], rsr.at[k], dev)

    def rs_arrive(rho, arr, g, way):
        k = (rho, arr, g, way)
        arrive(RSR.at[k], rsr.at[k])

    def row_b(rho, arr, g):
        arrive(XR.at[rho, arr, g], xr.at[rho, arr, g])
        for way, first in ((0, 0), (1, 3)):
            make = rs_pass(rho, arr, g, way)
            cond = zl == first
            for j in range(2):
                o = block_of(way, j)
                yy = shard_row(arr, g, o)
                s = PS[rho, arr, slot(o), c, yy] + XR[rho, arr, g, o].astype(F32)
                PS[rho, arr, slot(o), c, yy] = s

                @pl.when(cond)
                def _():
                    RSS[rho, arr, g, way, j] = s.astype(BF)

            send(make, cond)

    def row_c(rho, arr, g, hop, way):
        make = rs_pass(rho, arr, g, way)

        @pl.when(zl == (hop if way == 0 else 3 - hop))
        def _():
            rs_arrive(rho, arr, g, way)
            for j in range(2):
                o = block_of(way, j)
                s = PS[rho, arr, slot(o), c, shard_row(arr, g, o)] + RSR[rho, arr, g, way, j].astype(F32)
                RSS[rho, arr, g, way, j] = s.astype(BF)
            make().start()

    def row_sum(rho, arr, g, way):
        @pl.when(zl == (3 if way == 0 else 0))
        def _():
            rs_arrive(rho, arr, g, way)
            for j in range(2):
                o = block_of(way, j)
                yy = shard_row(arr, g, o)
                PS[rho, arr, slot(o), c, yy] = PS[rho, arr, slot(o), c, yy] + RSR[rho, arr, g, way, j].astype(F32)

    sent(XS, xss)
    sent(RSS.at[:, :, :, 0], rss.at[0], zl <= 2)
    sent(RSS.at[:, :, :, 1], rss.at[1], zl >= 1)
    sent(AD.at[:, 0:2, c], ads.at[0], zl <= 2)
    sent(AD.at[:, 2:4, c], ads.at[1], zl >= 1)
    sent(AD.at[:, :, c], acs)

    def ad_block(rho, o, yy, core):
        return AD.at[rho, o, core, yy]

    def ad_line(rho, way, k):
        dev = zp if way == 0 else zm
        ref = ad_block(rho, slot(block_of(1 - way, k // 4)), m4(y + k % 4), c)
        return lambda: rcopy(ref, ref, ads.at[way], adr.at[rho, way, k], dev)

    def ad_core(rho, o, yy):
        ref = ad_block(rho, o, yy, c)
        return lambda: rcopy(ref, ref, acs, acr.at[rho], co)

    def row_d(rho, k, way):
        o, yy = slot(block_of(way, k // 4)), m4(y + k % 4)
        line, core = ad_line(rho, 1 - way, k), ad_core(rho, o, yy)

        @pl.when(zl == (3 if way == 0 else 0))
        def _():
            pre = PS[rho, 0, o, c, yy]
            dact = PS[rho, 1, o, c, yy]
            cdf = 0.5 * (1.0 + lax.erf(pre * HALF_ROOT))
            dens = jnp.exp(-0.5 * pre * pre) * INV_ROOT_TAU
            AD[rho, o, c, yy, 0] = (pre * cdf).astype(BF)
            AD[rho, o, c, yy, 1] = (dact * (cdf + pre * dens)).astype(BF)
            line().start()
            core().start()

    def row_e(rho, k, hop, way):
        o, yy = slot(block_of(1 - way, k // 4)), m4(y + k % 4)
        line, core = ad_line(rho, way, k), ad_core(rho, o, yy)

        @pl.when(zl == (hop if way == 0 else 3 - hop))
        def _():
            arrive(ad_block(rho, o, yy, c), adr.at[rho, way, k])
            if hop < 3:
                line().start()
            core().start()

    def row_f(rho):
        arrive(AD.at[rho, :, oc], acr.at[rho])

    def ig_matmul(rho, h):
        @pl.loop(0, 3)
        def _(n):
            rows = pl.ds(pl.multiple_of(h * 768 + n * 256, 256), 256)
            cols = pl.ds(pl.multiple_of(n * 256, 256), 256)
            for o in range(0, 4, 2):
                dh = AD[rho, o:o + 2, :, :, 1].reshape(256, 768)
                acc = lax.dot_general(dh, U[rows, :], NT, preferred_element_type=F32)
                acc = acc.astype(BF).reshape(2, 2, 4, 16, 256)
                for oo in range(2):
                    for yy in range(4):
                        xx = (o + oo - yy) % 4
                        a, b = (yy, xx) if h == 0 else (xx, yy)
                        IG[rho, h, a, b, :, :, cols] = acc[oo, :, yy]

    class Scatter:
        def __init__(self, rho, h):
            self.rho, self.h = rho, h
            self.fp, self.fm, self.sp, self.sm = (yp, ym, xp, xm) if h == 0 else (xp, xm, yp, ym)
            self.a, self.b = (y, x) if h == 0 else (x, y)

            sent(IG.at[rho, h, 0:3], igs.at[rho, h, 0])
            sent(IG.at[rho, h, 0, 0:3], igs.at[rho, h, 1])

        slots = {0: 0, 1: 0, 2: 1, 3: 1, 4: 1, 5: 1, 6: 2, 7: 2, 8: 3, 9: 3, 10: 3, 11: 3}

        def put(self, k, src, dst, dev):
            ss, rs = igs.at[self.rho, self.h, 0 if k < 6 else 1], igr.at[self.rho, self.h, self.slots[k]]
            send(lambda: rcopy(src, dst, ss, rs, dev))

        def get(self, k, ref):
            arrive(ref, igr.at[self.rho, self.h, self.slots[k]])

        def start(self):
            i = (self.rho, self.h)
            a = self.a
            a2 = m4(a + 2)
            self.put(0, IG.at[i[0], i[1], a2, 0:2], RA.at[i[0], i[1], 0], self.fp)
            self.put(1, IG.at[i[0], i[1], a2, 2:4], RA.at[i[0], i[1], 1], self.fm)

        def start_b(self):
            i = (self.rho, self.h)
            a1, a3 = m4(self.a + 1), m4(self.a + 3)
            self.put(2, IG.at[i[0], i[1], a1, 2:4], RB.at[i[0], i[1], 0, 2:4], self.fp)
            self.put(3, IG.at[i[0], i[1], a3, 0:2], RB.at[i[0], i[1], 1, 0:2], self.fm)

        def step2(self):
            rho, h, a = self.rho, self.h, self.a
            a1, a3 = m4(a + 1), m4(a + 3)
            self.get(0, RA.at[rho, h])
            CS[rho, h, 0] = (IG[rho, h, a1, 0:2].astype(F32) + RA[rho, h, 0].astype(F32)).astype(BF)
            self.put(4, CS.at[rho, h, 0], RB.at[rho, h, 0, 0:2], self.fp)
            CS[rho, h, 1] = (IG[rho, h, a3, 2:4].astype(F32) + RA[rho, h, 1].astype(F32)).astype(BF)
            self.put(5, CS.at[rho, h, 1], RB.at[rho, h, 1, 2:4], self.fm)

        def step3(self):
            rho, h, a, b = self.rho, self.h, self.a, self.b
            self.get(2, RB.at[rho, h])
            for k in range(4):
                s = IG[rho, h, a, k].astype(F32) + RB[rho, h, 0, k].astype(F32) + RB[rho, h, 1, k].astype(F32)
                R1[rho, h, k] = s
                R1B[rho, h, k] = s.astype(BF)
            b1, b2, b3 = m4(b + 1), m4(b + 2), m4(b + 3)
            self.put(6, R1B.at[rho, h, b2, 0], RC.at[rho, h, 0], self.sp)
            self.put(7, R1B.at[rho, h, b2, 1], RC.at[rho, h, 1], self.sm)
            self.put(8, R1B.at[rho, h, b1, 1], RD.at[rho, h, 0, 1], self.sp)
            self.put(9, R1B.at[rho, h, b3, 0], RD.at[rho, h, 1, 0], self.sm)

        def step4(self):
            rho, h, b = self.rho, self.h, self.b
            b1, b3 = m4(b + 1), m4(b + 3)
            self.get(6, RC.at[rho, h])
            CS2[rho, h, 0] = (R1[rho, h, b1, 0] + RC[rho, h, 0].astype(F32)).astype(BF)
            self.put(10, CS2.at[rho, h, 0], RD.at[rho, h, 0, 0], self.sp)
            CS2[rho, h, 1] = (R1[rho, h, b3, 1] + RC[rho, h, 1].astype(F32)).astype(BF)
            self.put(11, CS2.at[rho, h, 1], RD.at[rho, h, 1, 1], self.sm)

        def step5(self):
            rho, h, b = self.rho, self.h, self.b
            self.get(8, RD.at[rho, h])
            s = R1[rho, h, b] + RD[rho, h, 0].astype(F32) + RD[rho, h, 1].astype(F32)
            if rho == 0:
                R2[h] = s
            else:
                ZS[h] = s.astype(BF)
                sent(ZS.at[h], zss.at[h])
                send(lambda: rcopy(ZS.at[h], ZR.at[h], zss.at[h], zsr.at[h], zz))

        def out(self):
            h = self.h
            arrive(ZR.at[h], zsr.at[h])
            OUT[:, h * 768:(h + 1) * 768] = (R2[h] + ZR[h].astype(F32)).astype(BF).reshape(32, 768)

    sc = [[Scatter(rho, h) for h in range(2)] for rho in range(2)]

    def mask_weights():
        @pl.loop(0, 12)
        def _(i):
            rows = pl.ds(pl.multiple_of(i * 128, 128), 128)
            for j in range(6):
                cols = slice(j * 128, (j + 1) * 128)
                m = upp[j, i].astype(F32)
                U[rows, cols] = (U[rows, cols].astype(F32) * m).astype(BF)

        @pl.loop(0, 12)
        def _(i):
            cols = pl.ds(pl.multiple_of(i * 128, 128), 128)
            for j in range(6):
                rows = slice(j * 128, (j + 1) * 128)
                m = dnp[j, i].astype(F32)
                DT[cols, rows] = (D[rows, cols].astype(F32) * m).T.astype(BF)

    factor = 1.0 / 32.0

    def up_grads(lo, hi):
        @pl.loop(lo, hi)
        def _(n):
            cols = pl.ds(pl.multiple_of(n * 256, 256), 256)
            t = T[:, :, :, :, :, cols].reshape(1024, 256)
            for f in range(3):
                dh = AD[:, :, :, :, 1, :, f * 256:(f + 1) * 256].reshape(1024, 256)
                res = lax.dot_general(t, dh, TN, preferred_element_type=F32)
                for bi in range(2):
                    for bj in range(2):
                        m = upp[f * 2 + bj, n * 2 + bi].astype(F32) * factor
                        UG[
                            pl.ds(pl.multiple_of(n * 256 + bi * 128, 128), 128),
                            f * 256 + bj * 128:f * 256 + (bj + 1) * 128,
                        ] = (res[bi * 128:(bi + 1) * 128, bj * 128:(bj + 1) * 128] * m).astype(BF)

    def down_grads(lo, hi):
        @pl.loop(lo, hi)
        def _(n):
            cols = pl.ds(pl.multiple_of(n * 256, 256), 256)
            g = G[:, :, :, :, :, cols].reshape(1024, 256)
            for f in range(3):
                ac = AD[:, :, :, :, 0, :, f * 256:(f + 1) * 256].reshape(1024, 256)
                res = lax.dot_general(ac, g, TN, preferred_element_type=F32)
                for bi in range(2):
                    for bj in range(2):
                        m = dnp[f * 2 + bi, n * 2 + bj].astype(F32) * factor
                        DG[
                            f * 256 + bi * 128:f * 256 + (bi + 1) * 128,
                            pl.ds(pl.multiple_of(n * 256 + bj * 128, 128), 128),
                        ] = (res[bi * 128:(bi + 1) * 128, bj * 128:(bj + 1) * 128] * m).astype(BF)

    def put_up(lo, hi):
        up_grads(lo, hi)
        rows = slice(lo * 256, hi * 256)
        pltpu.make_async_copy(UG.at[rows], ug_out.at[rows], lsem.at[4]).start()

    def put_down(lo, hi):
        down_grads(lo, hi)
        cols = slice(lo * 256, hi * 256)
        pltpu.make_async_copy(DG.at[:, cols], dg_out.at[:, cols], lsem.at[5]).start()

    steps = {}

    def at(name, fn, *args):
        steps[name] = (fn, args)

    def weights():
        locals_[2].wait()
        locals_[3].wait()
        mask_weights()

    for name, gt in (("g0t", gt0), ("g0g", gg0), ("g1t", gt1), ("g1g", gg1)):
        for step in ("start_a", "start_b", "step2a", "step2b", "step3", "step4a", "step4b", "step4c", "step4d", "near", "far"):
            at(name + "_" + step, getattr(gt, step))
    at("acrossT", across, T, 0)
    at("acrossG", across, G, 1)
    at("weights", weights)
    at("awaitT", across_wait, T, 0)
    at("awaitG", across_wait, G, 1)
    for rho in range(2):
        for g in range(4):
            for arr in range(2):
                n = "%d%d%d" % (rho, arr, g)
                at("a" + n, row_a, rho, arr, g)
                at("b" + n, row_b, rho, arr, g)
                for way, w in enumerate("rl"):
                    at("c1" + w + n, row_c, rho, arr, g, 1, way)
                    at("c2" + w + n, row_c, rho, arr, g, 2, way)
                    at("s" + w + n, row_sum, rho, arr, g, way)
        for k in range(8):
            n = "%d%d" % (rho, k)
            at("dr" + n, row_d, rho, k, 0)
            at("dl" + n, row_d, rho, k, 1)
            for hop in (1, 2, 3):
                at("e%dl" % hop + n, row_e, rho, k, hop, 0)
                at("e%dr" % hop + n, row_e, rho, k, hop, 1)
        at("f%d" % rho, row_f, rho)
        for h in range(2):
            n = "%d%d" % (rho, h)
            at("ig" + n, ig_matmul, rho, h)
            at("st" + n, sc[rho][h].start)
            at("sb" + n, sc[rho][h].start_b)
            for k in (2, 3, 4, 5):
                at("s%d" % k + n, getattr(sc[rho][h], "step%d" % k))
    for k in range(6):
        at("up%d" % k, put_up, k, k + 1)
        at("dn%d" % k, put_down, k, k + 1)
    at("out0", sc[0][0].out)
    at("out1", sc[0][1].out)

    names = list(steps)
    assert sorted(ORDER) == list(range(len(names)))
    for name in (names[k] for k in ORDER):
        fn, args = steps[name]
        with jax.named_scope(name):
            fn(*args)

    ig_copy = pltpu.make_async_copy(OUT, ig_out, lsem.at[0])
    ig_copy.start()

    with jax.named_scope("drain"):
        for cond, make in pending:
            if cond is None:
                make().wait_send()
            else:
                @pl.when(cond)
                def _():
                    make().wait_send()
    pltpu.make_async_copy(UG, ug_out, lsem.at[4]).wait()
    pltpu.make_async_copy(DG, dg_out, lsem.at[5]).wait()
    ig_copy.wait()


def on_device(tokens, up_weight, down_weight, cotangent, up_pattern, down_pattern):
    any_ = pl.BlockSpec(memory_space=pl.ANY)
    smem = pl.BlockSpec(memory_space=pltpu.SMEM)
    dma = pltpu.SemaphoreType.DMA
    V = pltpu.VMEM
    return pl.pallas_call(
        kernel,
        out_shape=(
            jax.ShapeDtypeStruct((32, 1536), BF),
            jax.ShapeDtypeStruct((1536, 768), BF),
            jax.ShapeDtypeStruct((768, 1536), BF),
        ),
        in_specs=[any_, any_, any_, any_, smem, smem],
        out_specs=(any_, any_, any_),
        scratch_shapes=[
            V((2, 4, 2, 4, 16, 1536), BF),
            V((2, 4, 2, 4, 16, 1536), BF),
            V((1536, 768), BF),
            V((768, 1536), BF),
            V((1536, 768), BF),
            V((2, 2, 4, 2, 4, 16, 768), F32),
            V((2, 2, 4, 4, 16, 768), BF),
            V((2, 2, 4, 4, 16, 768), BF),
            V((2, 2, 4, 2, 2, 16, 768), BF),
            V((2, 2, 4, 2, 2, 16, 768), BF),
            V((2, 4, 2, 4, 2, 16, 768), BF),
            V((2, 2, 4, 4, 2, 16, 768), BF),
            V((2, 2, 2, 2, 2, 16, 768), BF),
            V((2, 2, 2, 4, 2, 16, 768), BF),
            V((2, 2, 2, 2, 2, 16, 768), BF),
            V((2, 2, 4, 2, 16, 768), F32),
            V((2, 2, 4, 2, 16, 768), BF),
            V((2, 2, 2, 16, 768), BF),
            V((2, 2, 2, 2, 16, 768), BF),
            V((2, 2, 2, 16, 768), BF),
            V((2, 2, 16, 768), F32),
            V((2, 2, 16, 768), BF),
            V((2, 2, 16, 768), BF),
            V((1536, 768), BF),
            V((768, 1536), BF),
            V((32, 1536), BF),
            dma((7,)),
            dma((2, 2, 2)), dma((2, 2, 9)),
            dma((2,)), dma((2,)),
            dma, dma((2, 2, 4)),
            dma((2,)), dma((2, 2, 4, 2)),
            dma((2,)), dma((2, 2, 8)),
            dma, dma((2,)),
            dma((2, 2, 2)), dma((2, 2, 4)),
            dma((2,)), dma((2,)),
        ],
        compiler_params=pltpu.CompilerParams(
            collective_id=0, has_side_effects=True, vmem_limit_bytes=62 * 1024 * 1024
        ),
    )(
        tokens.reshape(2, 16, 1536),
        up_weight,
        down_weight,
        cotangent.reshape(2, 16, 1536),
        up_pattern.T,
        down_pattern,
    )


def solution(mesh):
    return jax.shard_map(
        on_device,
        mesh=mesh,
        in_specs=(
            P("col", "row"),
            P("row", "col"),
            P("col", "row"),
            P("col", "row"),
            P("row", "col"),
            P("col", "row"),
        ),
        out_specs=(P("col", "row"), P("row", "col"), P("col", "row")),
        check_vma=False,
    )
```

time: 137 us -> 109 us (0.80)
  Pallas kernels: 128 us -> 102 us
  local copies, waits for them, and re-layouts: 7.69 us -> 6.32 us
    pallas_call x1, Pallas kernels: 128 us -> 102 us  [on_device(): pl.pallas_call(kernel, out_shape=(jax.ShapeDtypeStruct((32, 1536), BF), j...]
    unnamed x6 -> x5, local copies, waits for them, and re-layouts: 7.69 us -> 6.32 us
where the time goes in v2:
time: 109 us
  Pallas kernels  102 us (94%)
  local copies, waits for them, and re-layouts  6.32 us (6%)
    pallas_call x1, Pallas kernels, on_device(): pl.pallas_call(kernel, out_shape=(jax.ShapeDtypeStruct((32, 1536), BF), j...  102 us
    unnamed x5, local copies, waits for them, and re-layouts  6.32 us

profile of v2, /device:TPU:2, one launch (start us, length us, event | category | flops | bytes accessed | tf_op | source)
XLA Modules:
  0.0 108.9 jit_solution(1483594477913882090)
XLA Ops:
  0.6 102.0 %shard_map.85 = (bf16[32,1536]{1,0:T(8,128)(2,1)}, bf16[1536,768]{1,0:T(8,128)(2,1)}, bf16[768,1536]{1,0:T(8,128)(2,1)}) custom-call(bf16[2,16,1536]{2,1,0:T(8,128)(2,1)} %bitcast.3, bf16[1536,768]{1,0:T(8,128)(2,1)} %upw.1, bf16[768,1536]{1,0:T(8,128)(2,1)} %dnw.1, bf16[2,16,1536]{2,1,0:T(8,128)(2,1)} %bitcast.4, s32[6,12]{1,0:T(8,128)} %bitcast.5, s32[6,12]{1,0:T(8,128)} %dnp.1), custom_call_target="tpu_custom_call" | custom-call | tf_op jit(solution)/shard_map/pallas_call | solution.py:538
  102.6 1.5 %copy.12 = bf16[32,1536]{1,0:T(8,128)(2,1)} copy(bf16[32,1536]{1,0:T(8,128)(2,1)} %get-tuple-element.6) | data formatting | bytes 196608
  104.1 0.0 copy-start
  104.1 3.4 %copy.13 = bf16[1536,768]{1,0:T(8,128)(2,1)} copy(bf16[1536,768]{1,0:T(8,128)(2,1)} %get-tuple-element.7) | data formatting | bytes 4718592
  107.5 0.0 copy-done
  107.5 1.4 %copy.14 = bf16[768,1536]{1,0:T(8,128)(2,1)} copy(bf16[768,1536]{1,0:T(8,128)(2,1)S(1)} %copy-done) | data formatting | bytes 4718592
Async XLA Ops:
  104.1 3.4 %copy-start = (bf16[768,1536]{1,0:T(8,128)(2,1)S(1)}, bf16[768,1536]{1,0:T(8,128)(2,1)}, u32[]{:S(2)}) copy-start(bf16[768,1536]{1,0:T(8,128)(2,1)} %get-tuple-element.8) | copy-start | bytes 7077892

commit v3 on v2

--- a/solution.py
+++ b/solution.py
@@ -33,8 +33,8 @@
 
 
 def kernel(
-    tok, upw, dnw, cot, upp, dnp, ig_out, ug_out, dg_out,
-    T, G, U, D, DT, PS, XS, XR, RSS, RSR, AD, IG, RA, RB, CS, R1, R1B, RC, RD, CS2, R2, ZS, ZR, UG, DG, OUT,
+    tok, upw, dnw, cot, upp, dnp, own_out, far_out, ug_out, dg_out,
+    T, G, U, D, DT, PS, XS, XR, RSS, RSR, AD, IG, RA, RB, CS, R1, R1B, RC, RD, CS2, R2, ZS, UG, DG,
     lsem, ags, agr, zxs, zxr, xss, xr, rss, rsr, ads, adr, acs, acr, igs, igr, zss, zsr,
 ):
     r = lax.axis_index("row")
@@ -383,17 +383,19 @@
             rho, h, b = self.rho, self.h, self.b
             self.get(8, RD.at[rho, h])
             s = R1[rho, h, b] + RD[rho, h, 0].astype(F32) + RD[rho, h, 1].astype(F32)
+            cols = slice(h * 768, (h + 1) * 768)
             if rho == 0:
-                R2[h] = s
+                R2[:, :, cols] = s
             else:
                 ZS[h] = s.astype(BF)
                 sent(ZS.at[h], zss.at[h])
-                send(lambda: rcopy(ZS.at[h], ZR.at[h], zss.at[h], zsr.at[h], zz))
+                send(lambda: rcopy(ZS.at[h], far_out.at[:, :, cols], zss.at[h], zsr.at[h], zz))
 
         def out(self):
             h = self.h
-            arrive(ZR.at[h], zsr.at[h])
-            OUT[:, h * 768:(h + 1) * 768] = (R2[h] + ZR[h].astype(F32)).astype(BF).reshape(32, 768)
+            if h == 0:
+                pltpu.make_async_copy(R2, own_out, lsem.at[0]).start()
+            arrive(far_out.at[:, :, h * 768:(h + 1) * 768], zsr.at[h])
 
     sc = [[Scatter(rho, h) for h in range(2)] for rho in range(2)]
 
@@ -514,9 +516,6 @@
         with jax.named_scope(name):
             fn(*args)
 
-    ig_copy = pltpu.make_async_copy(OUT, ig_out, lsem.at[0])
-    ig_copy.start()
-
     with jax.named_scope("drain"):
         for cond, make in pending:
             if cond is None:
@@ -527,7 +526,7 @@
                     make().wait_send()
     pltpu.make_async_copy(UG, ug_out, lsem.at[4]).wait()
     pltpu.make_async_copy(DG, dg_out, lsem.at[5]).wait()
-    ig_copy.wait()
+    pltpu.make_async_copy(R2, own_out, lsem.at[0]).wait()
 
 
 def on_device(tokens, up_weight, down_weight, cotangent, up_pattern, down_pattern):
@@ -535,15 +534,16 @@
     smem = pl.BlockSpec(memory_space=pltpu.SMEM)
     dma = pltpu.SemaphoreType.DMA
     V = pltpu.VMEM
-    return pl.pallas_call(
+    own, far, up_grad, down_grad = pl.pallas_call(
         kernel,
         out_shape=(
-            jax.ShapeDtypeStruct((32, 1536), BF),
+            jax.ShapeDtypeStruct((2, 16, 1536), F32),
+            jax.ShapeDtypeStruct((2, 16, 1536), BF),
             jax.ShapeDtypeStruct((1536, 768), BF),
             jax.ShapeDtypeStruct((768, 1536), BF),
         ),
         in_specs=[any_, any_, any_, any_, smem, smem],
-        out_specs=(any_, any_, any_),
+        out_specs=(any_, any_, any_, any_),
         scratch_shapes=[
             V((2, 4, 2, 4, 16, 1536), BF),
             V((2, 4, 2, 4, 16, 1536), BF),
@@ -565,12 +565,10 @@
             V((2, 2, 2, 16, 768), BF),
             V((2, 2, 2, 2, 16, 768), BF),
             V((2, 2, 2, 16, 768), BF),
-            V((2, 2, 16, 768), F32),
-            V((2, 2, 16, 768), BF),
+            V((2, 16, 1536), F32),
             V((2, 2, 16, 768), BF),
             V((1536, 768), BF),
             V((768, 1536), BF),
-            V((32, 1536), BF),
             dma((7,)),
             dma((2, 2, 2)), dma((2, 2, 9)),
             dma((2,)), dma((2,)),
@@ -592,6 +590,7 @@
         up_pattern.T,
         down_pattern,
     )
+    return ((own + far.astype(F32)).astype(BF).reshape(32, 1536), up_grad, down_grad)
 
 
 def solution(mesh):

time: 109 us -> 109 us (level)
  other arithmetic: 0 us -> 1.65 us
  local copies, waits for them, and re-layouts: 6.32 us -> 4.78 us
    convert_element_type x0 -> x1, other arithmetic: none -> 1.65 us  [on_device(): (own + far.astype(F32)).astype(BF).reshape(32, 1536)]
    unnamed x5 -> x4, local copies, waits for them, and re-layouts: 6.32 us -> 4.78 us
where the time goes in v3:
time: 109 us
  Pallas kernels  101 us (93%)
  local copies, waits for them, and re-layouts  4.78 us (4%)
  other arithmetic  1.65 us (2%)
    pallas_call x1, Pallas kernels, on_device(): pl.pallas_call(kernel, out_shape=(jax.ShapeDtypeStruct((2, 16, 1536), F32...  101 us
    unnamed x4, local copies, waits for them, and re-layouts  4.78 us

profile of v3, /device:TPU:2, one launch (start us, length us, event | category | flops | bytes accessed | tf_op | source)
XLA Modules:
  0.0 108.5 jit_solution(16265265927413690315)
XLA Ops:
  0.6 101.4 %shard_map.85 = (f32[2,16,1536]{2,1,0:T(8,128)}, bf16[2,16,1536]{2,1,0:T(8,128)(2,1)}, bf16[1536,768]{1,0:T(8,128)(2,1)}, bf16[768,1536]{1,0:T(8,128)(2,1)}) custom-call(bf16[2,16,1536]{2,1,0:T(8,128)(2,1)} %bitcast.5, bf16[1536,768]{1,0:T(8,128)(2,1)} %upw.1, bf16[768,1536]{1,0:T(8,128)(2,1)} %dnw.1, bf16[2,16,1536]{2,1,0:T(8,128)(2,1)} %bitcast.6, ...), custom_call_target="tpu_custom_call" | custom-call | tf_op jit(solution)/shard_map/pallas_call | solution.py:537
  102.1 1.7 %add_convert_fusion = bf16[2,16,1536]{2,1,0:T(8,128)(2,1)} fusion(f32[2,16,1536]{2,1,0:T(8,128)} %get-tuple-element.7, bf16[2,16,1536]{2,1,0:T(8,128)(2,1)} %get-tuple-element.8), kind=kLoop, calls=%fused_computation | loop fusion | flops 147456 | bytes 393216 | tf_op jit(solution)/shard_map/convert_element_type | solution.py:593
  103.7 0.0 copy-start
  103.7 3.4 %copy.11 = bf16[1536,768]{1,0:T(8,128)(2,1)} copy(bf16[1536,768]{1,0:T(8,128)(2,1)} %get-tuple-element.15) | data formatting | bytes 4718592
  107.1 0.0 copy-done
  107.1 1.4 %copy.12 = bf16[768,1536]{1,0:T(8,128)(2,1)} copy(bf16[768,1536]{1,0:T(8,128)(2,1)S(1)} %copy-done) | data formatting | bytes 4718592
Async XLA Ops:
  103.7 3.4 %copy-start = (bf16[768,1536]{1,0:T(8,128)(2,1)S(1)}, bf16[768,1536]{1,0:T(8,128)(2,1)}, u32[]{:S(2)}) copy-start(bf16[768,1536]{1,0:T(8,128)(2,1)} %get-tuple-element.16) | copy-start | bytes 7077892
